TPU v7x, 32 devices: a whole 2x2x4 slice. The times are simulated.
32 devices in a mesh: slab: 4 (over x, core), dir: 8 (over z, y).
Axes of the slice: x: 2, y: 2, z: 4, core: 2. Of those that a mesh axis runs over, the one named last changes fastest.
Arguments:
- currents: float32 [2, 64, 128, 256], P(None, ('slab', 'dir')), may hold values from -6 to 6
- near_blocks: float32 [2, 64, 9, 128, 128], P(None, ('slab', 'dir')), may hold values from -0.1875 to 0.1875
- near_index: int32 [64, 9], P(('slab', 'dir')), may hold values from 0 to 5
- aggregate: float32 [2, 256, 128], replicated, may hold values from -0.5 to 0.5
- translations: float32 [2, 64, 256], P(None, None, 'dir'), may hold values from -1 to 1
- inter_source: int32 [64, 32], P('slab'), may hold values from 0 to 47
- inter_shift: int32 [64, 32], P('slab'), may hold values from 0 to 63
- disaggregate: float32 [2, 128, 256], replicated, may hold values from -0.375 to 0.375
Outputs:
- product: float32 [2, 64, 128, 256], P(None, ('slab', 'dir'))
All inputs are finite; a program needn't handle non-finite values.
Results may differ from a plain program's by a relative error of at most 0.0003.
Values sent between devices are 32-bit elements; how exact they have to be, the bound alone decides.
A program may use at most 64 MiB of HBM per device.

v0:
```python
import functools

import jax
import jax.numpy as jnp
from jax import lax
from jax.experimental import pallas as pl
from jax.experimental.pallas import tpu as pltpu
from jax.sharding import PartitionSpec as P

MESH = pl.DeviceIdType.MESH
CHUNKS = 1


def split(x):
    hi = x.astype(jnp.bfloat16)
    lo = (x - hi.astype(jnp.float32)).astype(jnp.bfloat16)
    return hi, lo


def dot3(left, right):
    def single(u, v):
        return jnp.dot(u, v, preferred_element_type=jnp.float32)

    return single(left[0], right[0]) + (single(left[0], right[1]) + single(left[1], right[0]))


def complex_weights(real, imag):
    return jnp.concatenate(
        [jnp.concatenate([real, imag], axis=1), jnp.concatenate([-imag, real], axis=1)], axis=0
    )


def kernel(
    slabs, dirs, chunks,
    cur_hbm, near_hbm, near_index_hbm, aggregate_hbm, trans_hbm, source_hbm, shift_hbm, disaggregate_hbm,
    out,
    cur, near_index, aggregate, trans, inter_source, inter_shift, disaggregate, input_sem,
    near_blocks, near_hi, near_lo, near_src, near_turned, w_hi, w_lo,
    own_t, cells, trans_own, trans_all, rows, tables, agg_hi, agg_lo, dis_hi, dis_lo,
    x, inc, far_out, far_in,
    fwd_send, fwd_recv, slab_send, slab_recv, tr_send, tr_recv, ts_send, ts_recv,
    nb_send, nb_recv, ng_send, ng_recv, ret_send, ret_recv,
):
    slab = lax.axis_index("slab")
    me = lax.axis_index("dir")
    box_dev, p_size, illum = cur.shape[1:]
    nn = near_hbm.shape[2]
    k_size = aggregate.shape[1]
    nt = trans.shape[2]
    slab_boxes, ni = inter_source.shape
    rc = own_t.shape[4]
    rs = rc * chunks
    has_prev = slab > 0
    has_next = slab < slabs - 1
    shares = trans_all.shape[1]
    share = slab if shares > 1 else 0
    odd = lax.rem(me, 2)
    partner = me + 1 - 2 * odd

    def across(d):
        return lax.rem(d + 2 * lax.rem(d, 2) - 1 + dirs, dirs)

    barrier = pltpu.get_barrier_semaphore()

    @pl.loop(1, dirs)
    def _(o):
        pl.semaphore_signal(barrier, inc=1, device_id={"dir": lax.rem(me + o, dirs)}, device_id_type=MESH)

    @pl.loop(1, slabs)
    def _(o):
        pl.semaphore_signal(barrier, inc=1, device_id={"slab": lax.rem(slab + o, slabs)}, device_id_type=MESH)

    cur_copy, trans_copy, *later_copies = [
        pltpu.make_async_copy(source, target, input_sem.at[i])
        for i, (source, target) in enumerate([
            (cur_hbm, cur), (trans_hbm, trans), (aggregate_hbm, aggregate),
            (disaggregate_hbm, disaggregate), (source_hbm, inter_source),
            (shift_hbm, inter_shift), (near_index_hbm, near_index), (near_hbm, near_blocks),
        ])
    ]
    cur_copy.start()
    trans_copy.start()
    for copy in later_copies:
        copy.start()
    cur_copy.wait()

    for part in range(2):
        for b in range(box_dev):
            turned = cur[part, b].T
            for d in range(dirs):
                for c in range(chunks):
                    start = d * rs + c * rc
                    own_t[c, d, part, b] = turned[start:start + rc]
    trans_copy.wait()
    trans_own[...] = jnp.concatenate([trans[0], trans[1]], axis=1).reshape(trans_own.shape)

    pl.semaphore_wait(barrier, dirs + slabs - 2)

    def fwd_copy(c, peer, slot):
        return pltpu.make_async_remote_copy(
            src_ref=own_t.at[c, peer], dst_ref=cells.at[c, 1, slot],
            send_sem=fwd_send.at[c, peer], recv_sem=fwd_recv.at[c, slot],
            device_id={"dir": peer}, device_id_type=MESH,
        )

    def tr_copy(peer, slot):
        return pltpu.make_async_remote_copy(
            src_ref=trans_own.at[share], dst_ref=trans_all.at[slot, share],
            send_sem=tr_send.at[peer], recv_sem=tr_recv.at[slot],
            device_id={"dir": peer}, device_id_type=MESH,
        )

    def ts_copy(peer, slot):
        return pltpu.make_async_remote_copy(
            src_ref=trans_all.at[:, slot], dst_ref=trans_all.at[:, slot],
            send_sem=ts_send.at[peer], recv_sem=ts_recv.at[slot],
            device_id={"slab": peer}, device_id_type=MESH,
        )

    def ng_copy(c, d, slot):
        return pltpu.make_async_remote_copy(
            src_ref=cells.at[c, 1, d], dst_ref=near_turned.at[c, slot],
            send_sem=ng_send.at[c, d], recv_sem=ng_recv.at[c, slot],
            device_id={"dir": across(d)}, device_id_type=MESH,
        )

    def slab_copy(c, side, d):
        target = slab + 1 if side == 0 else slab - 1
        return pltpu.make_async_remote_copy(
            src_ref=cells.at[c, 1, d], dst_ref=cells.at[c, 2 * side, d],
            send_sem=slab_send.at[c, side, d], recv_sem=slab_recv.at[c, side, d],
            device_id={"slab": target}, device_id_type=MESH,
        )

    def nb_copy():
        return pltpu.make_async_remote_copy(
            src_ref=cur, dst_ref=near_src, send_sem=nb_send, recv_sem=nb_recv,
            device_id={"dir": partner}, device_id_type=MESH,
        )

    def ret_copy(c, peer, slot):
        return pltpu.make_async_remote_copy(
            src_ref=far_out.at[c, peer], dst_ref=far_in.at[c, slot],
            send_sem=ret_send.at[c, peer], recv_sem=ret_recv.at[c, slot],
            device_id={"dir": peer}, device_id_type=MESH,
        )

    def forward(c, d):
        @pl.when(has_next)
        def _():
            slab_copy(c, 0, d).start()

        @pl.when(has_prev)
        def _():
            slab_copy(c, 1, d).start()

        @pl.when(across(d) != me)
        def _():
            ng_copy(c, d, me).start()

    @pl.loop(1, dirs)
    def _(o):
        tr_copy(lax.rem(me + o, dirs), me).start()

    for c in range(chunks):
        @pl.loop(1, dirs)
        def _(o):
            peer = lax.rem(me + o, dirs)
            fwd_copy(c, peer, me).start()

    nb_copy().start()

    for c in range(chunks):
        cells[c, 1, me] = own_t[c, me]
        forward(c, me)

    trans_all[me, share] = trans_own[share]

    @pl.when(jnp.logical_not(has_prev))
    def _():
        cells[:, 0] = jnp.zeros_like(cells[:, 0])

    @pl.when(jnp.logical_not(has_next))
    def _():
        cells[:, 2] = jnp.zeros_like(cells[:, 2])

    for copy in later_copies:
        copy.wait()
    agg_hi[...], agg_lo[...] = split(complex_weights(aggregate[0].T, aggregate[1].T))
    dis_hi[...], dis_lo[...] = split(complex_weights(disaggregate[0].T, disaggregate[1].T))

    @pl.loop(1, dirs)
    def _(o):
        peer = lax.rem(me + dirs - o, dirs)
        tr_copy(peer, peer).wait_recv()

    if shares > 1:
        @pl.loop(1, slabs)
        def _(o):
            ts_copy(lax.rem(slab + o, slabs), slab).start()

    for b in range(box_dev):
        @pl.loop(0, nn)
        def _(j):
            pair = jnp.concatenate([near_blocks[0, b, j], near_blocks[1, b, j]], axis=1)
            near_hi[b, j], near_lo[b, j] = split(pair)

    def radiate(c, g):
        count = dirs * box_dev * rc
        pair = jnp.concatenate(
            [cells[c, g, :, part].reshape(count, p_size) for part in range(2)], axis=1
        )
        y = dot3(split(pair), (agg_hi[...], agg_lo[...]))
        re = y[:, :k_size].reshape(slab_boxes, rc // 8, 8, k_size)
        im = y[:, k_size:].reshape(slab_boxes, rc // 8, 8, k_size)
        boxes = pl.ds(g * slab_boxes, slab_boxes)
        x[0, boxes] = re
        x[1, boxes] = im
        x[2, boxes] = re + im

    def far_device(c, owner):
        for bb in range(box_dev):
            b = owner * box_dev + bb

            def entry(i, sums):
                s1, s2, s3 = sums
                src = inter_source[b, i]
                shift = inter_shift[b, i]
                s1 = s1 + tables[0, shift] * x[2, src]
                s2 = s2 + tables[1, shift] * x[1, src]
                s3 = s3 + tables[2, shift] * x[0, src]
                return s1, s2, s3

            zero = jnp.zeros((rc // 8, 8, k_size), jnp.float32)
            s1, s2, s3 = lax.fori_loop(0, ni, entry, (zero, zero, zero), unroll=4)
            here = slice(bb * rc, (bb + 1) * rc)
            inc[here, :k_size] = (s1 - s2).reshape(rc, k_size)
            inc[here, k_size:] = (s1 + s3).reshape(rc, k_size)
        y = dot3(split(inc[...]), (dis_hi[...], dis_lo[...]))
        far_out[c, owner, 0] = y[:, :p_size].reshape(box_dev, rc, p_size)
        far_out[c, owner, 1] = y[:, p_size:].reshape(box_dev, rc, p_size)

    for c in range(chunks):
        @pl.loop(1, dirs)
        def _(o):
            peer = lax.rem(me + dirs - o, dirs)
            fwd_copy(c, peer, peer).wait_recv()
            forward(c, peer)

        if c == 0:
            if shares > 1:
                @pl.loop(1, slabs)
                def _(o):
                    peer = lax.rem(slab + slabs - o, slabs)
                    ts_copy(peer, peer).wait_recv()

            turned = trans_all[...].reshape(k_size, 2 * nt).T
            rows[0] = turned[:nt]
            rows[1] = turned[:nt] + turned[nt:]
            rows[2] = turned[nt:] - turned[:nt]

            @pl.loop(0, nt)
            def _(t):
                for f in range(3):
                    tables[f, t] = jnp.broadcast_to(rows[f, pl.ds(t, 1), :], (8, k_size))

        radiate(c, 1)

        @pl.when(has_prev)
        def _():
            @pl.loop(0, dirs)
            def _(d):
                slab_copy(c, 0, d).wait_recv()

        radiate(c, 0)

        @pl.when(has_next)
        def _():
            @pl.loop(0, dirs)
            def _(d):
                slab_copy(c, 1, d).wait_recv()

        radiate(c, 2)

        @pl.loop(1, dirs + 1)
        def _(o):
            owner = lax.rem(me + o, dirs)
            far_device(c, owner)

            @pl.when(o < dirs)
            def _():
                ret_copy(c, owner, me).start()

        far_in[c, me] = far_out[c, me]

    def near_weights(group, b, real, imag):
        w_hi[group * box_dev + b], w_lo[group * box_dev + b] = split(complex_weights(real, imag))

    def whole(ref, part, b):
        pieces = [ref[c, d, part, b] for d in range(dirs) for c in range(chunks)]
        return jnp.concatenate(pieces, axis=0).T

    nb_copy().wait_recv()
    for b in range(box_dev):
        near_weights(1, b, cur[0, b], cur[1, b])
        near_weights(2 - 2 * odd, b, near_src[0, b], near_src[1, b])

    for c in range(chunks):
        near_turned[c, me] = cells[c, 1, across(me)]

        @pl.loop(1, dirs)
        def _(o):
            slot = lax.rem(me + dirs - o, dirs)
            ng_copy(c, across(me), slot).wait_recv()

    for b in range(box_dev):
        near_weights(2 * odd, b, whole(near_turned, 0, b), whole(near_turned, 1, b))

    @pl.loop(0, box_dev)
    def _(b):
        total = jnp.zeros((p_size, 2 * illum), jnp.float32)
        for j in range(nn):
            src = near_index[b, j]
            total = total + dot3((near_hi[b, j], near_lo[b, j]), (w_hi[src], w_lo[src]))
        out[0, b] = total[:, :illum]
        out[1, b] = total[:, illum:]

    for c in range(chunks):
        @pl.loop(1, dirs)
        def _(o):
            peer = lax.rem(me + dirs - o, dirs)
            ret_copy(c, peer, peer).wait_recv()

    for part in range(2):
        for b in range(box_dev):
            out[part, b] += whole(far_in, part, b)

    for c in range(chunks):
        @pl.loop(1, dirs)
        def _(o):
            peer = lax.rem(me + o, dirs)
            fwd_copy(c, peer, me).wait_send()
            ret_copy(c, peer, me).wait_send()
            if c == 0:
                tr_copy(peer, me).wait_send()

        @pl.loop(0, dirs)
        def _(d):
            @pl.when(across(d) != me)
            def _():
                ng_copy(c, d, me).wait_send()

        @pl.when(has_next)
        def _():
            @pl.loop(0, dirs)
            def _(d):
                slab_copy(c, 0, d).wait_send()

        @pl.when(has_prev)
        def _():
            @pl.loop(0, dirs)
            def _(d):
                slab_copy(c, 1, d).wait_send()

    if shares > 1:
        @pl.loop(1, slabs)
        def _(o):
            ts_copy(lax.rem(slab + o, slabs), slab).wait_send()

    nb_copy().wait_send()


def body(slabs, dirs, *args):
    cur, near_blocks, near_index, aggregate, trans, inter_source, inter_shift, disaggregate = args
    box_dev, p_size, illum = cur.shape[1:]
    nn = near_blocks.shape[2]
    k_size = aggregate.shape[1]
    nt, k_loc = trans.shape[1:]
    slab_boxes = inter_source.shape[0]
    rs = illum // dirs
    chunks = CHUNKS if rs % (8 * CHUNKS) == 0 else 1
    rc = rs // chunks
    shares = slabs if k_loc % (8 * slabs) == 0 else 1
    f32, bf16 = jnp.float32, jnp.bfloat16
    vmem = pl.BlockSpec(memory_space=pltpu.VMEM)
    sem = pltpu.SemaphoreType.DMA
    return pl.pallas_call(
        functools.partial(kernel, slabs, dirs, chunks),
        out_shape=jax.ShapeDtypeStruct(cur.shape, f32),
        in_specs=[pl.BlockSpec(memory_space=pltpu.HBM)] * 8,
        out_specs=vmem,
        scratch_shapes=[
            pltpu.VMEM(cur.shape, f32),
            pltpu.SMEM(near_index.shape, jnp.int32),
            pltpu.VMEM(aggregate.shape, f32),
            pltpu.VMEM((2, k_loc, nt), f32),
            pltpu.SMEM(inter_source.shape, jnp.int32),
            pltpu.SMEM(inter_shift.shape, jnp.int32),
            pltpu.VMEM(disaggregate.shape, f32),
            sem((8,)),
            pltpu.VMEM(near_blocks.shape, f32),
            pltpu.VMEM((box_dev, nn, p_size, 2 * p_size), bf16),
            pltpu.VMEM((box_dev, nn, p_size, 2 * p_size), bf16),
            pltpu.VMEM(cur.shape, f32),
            pltpu.VMEM((chunks, dirs, 2, box_dev, rc, p_size), f32),
            pltpu.VMEM((3 * box_dev, 2 * p_size, 2 * illum), bf16),
            pltpu.VMEM((3 * box_dev, 2 * p_size, 2 * illum), bf16),
            pltpu.VMEM((chunks, dirs, 2, box_dev, rc, p_size), f32),
            pltpu.VMEM((chunks, 3, dirs, 2, box_dev, rc, p_size), f32),
            pltpu.VMEM((shares, k_loc // shares, 2 * nt), f32),
            pltpu.VMEM((dirs, shares, k_loc // shares, 2 * nt), f32),
            pltpu.VMEM((3, nt, k_size), f32),
            pltpu.VMEM((3, nt, 8, k_size), f32),
            pltpu.VMEM((2 * p_size, 2 * k_size), bf16),
            pltpu.VMEM((2 * p_size, 2 * k_size), bf16),
            pltpu.VMEM((2 * k_size, 2 * p_size), bf16),
            pltpu.VMEM((2 * k_size, 2 * p_size), bf16),
            pltpu.VMEM((3, 3 * slab_boxes, rc // 8, 8, k_size), f32),
            pltpu.VMEM((box_dev * rc, 2 * k_size), f32),
            pltpu.VMEM((chunks, dirs, 2, box_dev, rc, p_size), f32),
            pltpu.VMEM((chunks, dirs, 2, box_dev, rc, p_size), f32),
            sem((chunks, dirs)), sem((chunks, dirs)),
            sem((chunks, 2, dirs)), sem((chunks, 2, dirs)),
            sem((dirs,)), sem((dirs,)),
            sem((slabs,)), sem((slabs,)),
            sem(()), sem(()),
            sem((chunks, dirs)), sem((chunks, dirs)),
            sem((chunks, dirs)), sem((chunks, dirs)),
        ],
        compiler_params=pltpu.CompilerParams(
            collective_id=0, has_side_effects=True, vmem_limit_bytes=60 * 2**20
        ),
    )(cur, near_blocks, near_index, aggregate, jnp.swapaxes(trans, 1, 2), inter_source, inter_shift, disaggregate)


def solution(mesh):
    in_specs = (
        P(None, ("slab", "dir"), None, None),
        P(None, ("slab", "dir"), None, None, None),
        P(("slab", "dir"), None),
        P(),
        P(None, None, "dir"),
        P("slab", None),
        P("slab", None),
        P(),
    )
    out_specs = P(None, ("slab", "dir"), None, None)
    run = functools.partial(body, mesh.shape["slab"], mesh.shape["dir"])
    return jax.shard_map(run, mesh=mesh, in_specs=in_specs, out_specs=out_specs, check_vma=False)
```

profile of v0, /device:TPU:15, one launch (start us, length us, event | category | flops | bytes accessed | tf_op | source)
XLA Modules:
  0.0 43.4 jit_solution(12321243077176157227)
XLA Ops:
  0.0 41.5 %shard_map.82 = f32[2,2,128,256]{3,2,1,0:T(8,128)} custom-call(f32[2,2,128,256]{3,2,1,0:T(8,128)} %cur_hbm.1, f32[2,2,9,128,128]{4,3,2,1,0:T(8,128)} %near_hbm.1, s32[2,9]{1,0:T(2,128)} %near_index_hbm.1, f32[2,256,128]{2,1,0:T(8,128)} %aggregate_hbm.1, f32[2,32,64]{2,1,0:T(8,128)} %bitcast.1, s32[16,32]{1,0:T(8,128)} %source_hbm.1, s32[16,32]{1,0:T(8,128)} %shift_hbm.1, ...), custom_call_target="tpu_custom_call" | custom-call | tf_op jit(solution)/shard_map/pallas_call | solution.py:387
  41.5 1.9 %copy.10 = f32[2,2,128,256]{3,2,1,0:T(8,128)} copy(f32[2,2,128,256]{3,2,1,0:T(8,128)} %shard_map.82) | data formatting | bytes 1048576
where the time goes:
time: 43.5 us; the launch traced here: 43.4 us
  Pallas kernels  41.5 us (95%)
  local copies, waits for them, and re-layouts  1.87 us (4%)
    pallas_call x1, Pallas kernels, body(): pl.pallas_call(functools.partial(kernel, slabs, dirs, chunks), out_shape=...  41.5 us
    unnamed x1, local copies, waits for them, and re-layouts  1.87 us

commit v1 on v0

--- a/solution.py
+++ b/solution.py
@@ -428,9 +428,10 @@
             sem((chunks, dirs)), sem((chunks, dirs)),
         ],
         compiler_params=pltpu.CompilerParams(
-            collective_id=0, has_side_effects=True, vmem_limit_bytes=60 * 2**20
+            collective_id=0, has_side_effects=True, vmem_limit_bytes=48 * 2**20
         ),
-    )(cur, near_blocks, near_index, aggregate, jnp.swapaxes(trans, 1, 2), inter_source, inter_shift, disaggregate)
+    )(*[pltpu.with_memory_space_constraint(v, pltpu.HBM) for v in (
+        cur, near_blocks, near_index, aggregate, jnp.swapaxes(trans, 1, 2), inter_source, inter_shift, disaggregate)])
 
 
 def solution(mesh):

time: 43.5 us -> 41.7 us (0.959)
  local copies, waits for them, and re-layouts: 1.87 us -> 0.8 us
  Pallas kernels: 41.5 us -> 40.7 us
    unnamed x1, local copies, waits for them, and re-layouts: 1.87 us -> 0.8 us
    pallas_call x1, Pallas kernels: 41.5 us -> 40.7 us  [body(): pl.pallas_call(functools.partial(kernel, slabs, dirs, chunks), out_shape=...]
where the time goes in v1:
time: 41.7 us; the launch traced here: 41.5 us
  Pallas kernels  40.7 us (98%)
  local copies, waits for them, and re-layouts  0.8 us (2%)
    pallas_call x1, Pallas kernels, body(): pl.pallas_call(functools.partial(kernel, slabs, dirs, chunks), out_shape=...  40.7 us

profile of v1, /device:TPU:15, one launch (start us, length us, event | category | flops | bytes accessed | tf_op | source)
XLA Modules:
  0.0 41.5 jit_solution(16435463458690532231)
XLA Ops:
  0.0 40.7 %shard_map.82 = f32[2,2,128,256]{3,2,1,0:T(8,128)S(1)} custom-call(f32[2,2,128,256]{3,2,1,0:T(8,128)} %cur_hbm.1, f32[2,2,9,128,128]{4,3,2,1,0:T(8,128)} %near_hbm.1, s32[2,9]{1,0:T(2,128)} %near_index_hbm.1, f32[2,256,128]{2,1,0:T(8,128)} %aggregate_hbm.1, f32[2,32,64]{2,1,0:T(8,128)} %bitcast.1, s32[16,32]{1,0:T(8,128)} %source_hbm.1, s32[16,32]{1,0:T(8,128)} %shift_hbm.1, ...), custom_call_target="tpu_custom_call" | custom-call | tf_op jit(solution)/shard_map/pallas_call | solution.py:387
  40.7 0.8 %copy.10 = f32[2,2,128,256]{3,2,1,0:T(8,128)} copy(f32[2,2,128,256]{3,2,1,0:T(8,128)S(1)} %shard_map.82) | data formatting | bytes 1048576

commit v2 on v1

v2 whole, which is shorter than its diff:
```python
import functools

import jax
import jax.numpy as jnp
from jax import lax
from jax.experimental import pallas as pl
from jax.experimental.pallas import tpu as pltpu
from jax.sharding import PartitionSpec as P

MESH = pl.DeviceIdType.MESH


def split(x):
    hi = x.astype(jnp.bfloat16)
    lo = (x - hi.astype(jnp.float32)).astype(jnp.bfloat16)
    return hi, lo


def dot3(left, right):
    def single(u, v):
        return jnp.dot(u, v, preferred_element_type=jnp.float32)

    return single(left[0], right[0]) + (single(left[0], right[1]) + single(left[1], right[0]))


def complex_weights(real, imag):
    return jnp.concatenate(
        [jnp.concatenate([real, imag], axis=1), jnp.concatenate([-imag, real], axis=1)], axis=0
    )


def plan(illum, zs):
    half = illum // 2
    return ((zs, half // zs, 0),)


def kernel(
    slabs, dirs, chunks,
    cur_hbm, near_hbm, near_index_hbm, aggregate_hbm, trans_hbm, source_hbm, shift_hbm, disaggregate_hbm,
    out,
    cur, near_index, aggregate, trans, inter_source, inter_shift, disaggregate, input_sem,
    near_blocks, near_hi, near_lo, near_par, near_turned, w_hi, w_lo,
    own_t, par_t, far_all, trans_own, trans_all, rows, tables, agg_hi, agg_lo, dis_hi, dis_lo,
    cells, x, inc, far_out,
    hand, first_send, first_recv, line_send, relay_send, line_recv, slab_send, slab_recv,
    tr_send, tr_recv, ts_send, ts_recv, nb_send, nb_recv, ng_send, ng_recv,
    na_send, na_recv, nr_send, nr_recv, ret_send, ret_recv,
):
    slab = lax.axis_index("slab")
    me = lax.axis_index("dir")
    box_dev, p_size, illum = cur.shape[1:]
    nn = near_hbm.shape[2]
    k_size = aggregate.shape[1]
    nt = trans.shape[2]
    slab_boxes, ni = inter_source.shape
    has_prev = slab > 0
    has_next = slab < slabs - 1
    shares = trans_all.shape[1]
    share = slab if shares > 1 else 0
    zs = dirs // 2
    zh = zs // 2
    hr = illum // 2
    z = me // 2
    y = lax.rem(me, 2)
    partner = 2 * z + 1 - y
    has_lower = z > 0
    has_upper = z < zs - 1
    inward = 1 - 2 * (z // zh)

    def toward(o):
        return lax.rem(z + inward * o + zs, zs)

    def across(d):
        return lax.rem(d + 2 * lax.rem(d, 2) - 1 + dirs, dirs)

    def row(c, side, i):
        nz, rc, off = chunks[c]
        return pl.multiple_of(side * hr + off + lax.rem(i, nz) * rc, 8)

    def my_rows(c, side, i):
        return pl.ds(row(c, side, i), chunks[c][1])

    barrier = pltpu.get_barrier_semaphore()

    def greet(sem, peer):
        pl.semaphore_signal(sem, inc=1, device_id={"dir": peer}, device_id_type=MESH)

    greet(barrier, partner)

    @pl.when(has_lower)
    def _():
        greet(barrier, me - 2)

    @pl.when(has_upper)
    def _():
        greet(barrier, me + 2)

    @pl.loop(1, slabs)
    def _(o):
        pl.semaphore_signal(barrier, inc=1, device_id={"slab": lax.rem(slab + o, slabs)}, device_id_type=MESH)

    cur_copy, trans_copy, *later_copies = [
        pltpu.make_async_copy(source, target, input_sem.at[i])
        for i, (source, target) in enumerate([
            (cur_hbm, cur), (trans_hbm, trans), (aggregate_hbm, aggregate),
            (disaggregate_hbm, disaggregate), (source_hbm, inter_source),
            (shift_hbm, inter_shift), (near_index_hbm, near_index), (near_hbm, near_blocks),
        ])
    ]
    cur_copy.start()
    trans_copy.start()
    for copy in later_copies:
        copy.start()
    cur_copy.wait()

    for part in range(2):
        for b in range(box_dev):
            own_t[part, b] = cur[part, b].T
    trans_copy.wait()
    trans_own[...] = jnp.concatenate([trans[0], trans[1]], axis=1).reshape(trans_own.shape)

    def remote(src, dst, send, recv, **peer):
        return pltpu.make_async_remote_copy(
            src_ref=src, dst_ref=dst, send_sem=send, recv_sem=recv, device_id=peer, device_id_type=MESH
        )

    def first_copy(c, i, side):
        return remote(
            own_t.at[:, :, my_rows(c, side, i)], par_t.at[:, :, my_rows(c, 0, i)],
            first_send.at[c, i], first_recv.at[c, i], dir=partner,
        )

    def line_copy(c, peer, slot):
        return remote(
            own_t.at[:, :, my_rows(c, y, peer // 2)], cells[c].at[1, slot],
            line_send.at[c, peer // 2], line_recv.at[c, slot], dir=peer,
        )

    def relay_copy(c, peer, slot):
        return remote(
            par_t.at[:, :, my_rows(c, 0, peer // 2)], cells[c].at[1, slot],
            relay_send.at[c, peer // 2], line_recv.at[c, slot], dir=peer,
        )

    def tr_copy(peer, slot):
        return remote(
            trans_own.at[share], trans_all.at[slot, share], tr_send.at[peer], tr_recv.at[slot], dir=peer
        )

    def ts_copy(peer, slot):
        return remote(
            trans_all.at[:, slot], trans_all.at[:, slot], ts_send.at[peer], ts_recv.at[slot], slab=peer
        )

    def slab_copy(c, side, d):
        target = slab + 1 if side == 0 else slab - 1
        return remote(
            cells[c].at[1, d], cells[c].at[2 * side, d],
            slab_send.at[c, side, d], slab_recv.at[c, side, d], slab=target,
        )

    def nb_copy(side):
        lanes = pl.ds(pl.multiple_of(side * hr, 128), hr)
        return remote(
            cur.at[:, :, :, lanes], near_par.at[:, :, :, lanes], nb_send, nb_recv, dir=partner
        )

    def ng_copy(c, d, holder):
        return remote(
            cells[c].at[1, d], near_turned.at[:, :, my_rows(c, lax.rem(holder, 2), holder // 2)],
            ng_send.at[c, d], ng_recv.at[c, holder], dir=across(d),
        )

    def apart(c, side, target):
        nz, rc, off = chunks[c]
        start = off + (1 - target // 2 // zh) * zh * rc
        return pl.ds(pl.multiple_of(side * hr + start, 8), zh * rc)

    def na_copy(c, side, target, peer):
        window = apart(c, side, target)
        return remote(
            own_t.at[:, :, window], near_turned.at[:, :, window], na_send.at[c], na_recv.at[c], dir=peer
        )

    def nr_copy(c, side, target, peer):
        return remote(
            par_t.at[:, :, apart(c, 0, target)], near_turned.at[:, :, apart(c, side, target)],
            nr_send.at[c], nr_recv.at[c], dir=peer,
        )

    def ret_copy(c, peer, sender):
        return remote(
            far_out[c].at[peer], far_all.at[:, :, my_rows(c, lax.rem(sender, 2), sender // 2)],
            ret_send.at[c, peer], ret_recv.at[c, sender], dir=peer,
        )

    def same_half(d):
        return d // 2 // zh == z // zh

    def passes_on(d):
        return jnp.logical_and(same_half(across(d)), across(d) != me)

    def forward(c, d):
        @pl.when(has_next)
        def _():
            slab_copy(c, 0, d).start()

        @pl.when(has_prev)
        def _():
            slab_copy(c, 1, d).start()

    def stage(s):
        @pl.when(has_upper)
        def _():
            greet(hand.at[s, 0], me + 2)

        @pl.when(has_lower)
        def _():
            greet(hand.at[s, 1], me - 2)

    def staged(s):
        @pl.when(has_lower)
        def _():
            pl.semaphore_wait(hand.at[s, 0], 1)

        @pl.when(has_upper)
        def _():
            pl.semaphore_wait(hand.at[s, 1], 1)

    def along(o):
        @pl.when(z + o < zs)
        def _():
            tr_copy(me + 2 * o, me).start()
            for c in range(len(chunks)):
                line_copy(c, me + 2 * o, me).start()

        @pl.when(z - o >= 0)
        def _():
            tr_copy(me - 2 * o, me).start()
            for c in range(len(chunks)):
                line_copy(c, me - 2 * o, me).start()

    def askew(o):
        @pl.when(z + o < zs)
        def _():
            tr_copy(partner + 2 * o, me).start()

        @pl.when(z - o >= 0)
        def _():
            tr_copy(partner - 2 * o, me).start()

    pl.semaphore_wait(barrier, slabs + (z + zs - 1) // zs + (2 * zs - 2 - z) // zs)
    stage(0)
    for c, (nz, rc, off) in enumerate(chunks):
        for o in range(nz):
            first_copy(c, lax.rem(toward(o + 1), nz), 1 - y).start()
    tr_copy(partner, me).start()
    along(1)
    nb_copy(y).start()
    for c in range(len(chunks)):
        cells[c][1, me] = own_t[:, :, my_rows(c, y, z)]
        forward(c, me)
    for o in range(2, zs):
        staged(o - 2)
        stage(o - 1)
        askew(o - 1)
        along(o)
    staged(zs - 2)
    askew(zs - 1)

    for copy in later_copies:
        copy.wait()
    agg_hi[...], agg_lo[...] = split(complex_weights(aggregate[0].T, aggregate[1].T))
    dis_hi[...], dis_lo[...] = split(complex_weights(disaggregate[0].T, disaggregate[1].T))

    for c, (nz, rc, off) in enumerate(chunks):
        for o in range(nz):
            i = lax.rem(toward(o + 1), nz)
            first_copy(c, i, 1 - y).wait_recv()
            for g in range(zs // nz):
                @pl.when(i + g * nz != z)
                def _():
                    relay_copy(c, 2 * (i + g * nz) + y, partner).start()

        cells[c][1, partner] = par_t[:, :, my_rows(c, 0, z)]
        forward(c, partner)

    trans_all[me, share] = trans_own[share]

    @pl.when(jnp.logical_not(has_prev))
    def _():
        for c in range(len(chunks)):
            cells[c][0] = jnp.zeros_like(cells[c][0])

    @pl.when(jnp.logical_not(has_next))
    def _():
        for c in range(len(chunks)):
            cells[c][2] = jnp.zeros_like(cells[c][2])

    @pl.loop(1, dirs)
    def _(o):
        peer = lax.rem(me + dirs - o, dirs)
        tr_copy(peer, peer).wait_recv()

    if shares > 1:
        @pl.loop(1, slabs)
        def _(o):
            ts_copy(lax.rem(slab + o, slabs), slab).start()

    steps = 2 * (zs - 1) * len(chunks)
    load = -(-box_dev * nn // steps)

    def split_near(t):
        @pl.loop(t * load, jnp.minimum((t + 1) * load, box_dev * nn))
        def _(q):
            b, j = q // nn, lax.rem(q, nn)
            pair = jnp.concatenate([near_blocks[0, b, j], near_blocks[1, b, j]], axis=1)
            near_hi[b, j], near_lo[b, j] = split(pair)

    def radiate(c, g):
        rc = chunks[c][1]
        count = dirs * box_dev * rc
        pair = jnp.concatenate(
            [cells[c][g, :, part].reshape(count, p_size) for part in range(2)], axis=1
        )
        w = dot3(split(pair), (agg_hi[...], agg_lo[...]))
        re = w[:, :k_size].reshape(slab_boxes, rc // 8, 8, k_size)
        im = w[:, k_size:].reshape(slab_boxes, rc // 8, 8, k_size)
        boxes = pl.ds(g * slab_boxes, slab_boxes)
        x[c][0, boxes] = re
        x[c][1, boxes] = im
        x[c][2, boxes] = re + im

    def far_device(c, owner):
        rc = chunks[c][1]
        step = min(rc // 8, 4)
        for bb in range(box_dev):
            b = owner * box_dev + bb
            for r in range(0, rc // 8, step):
                block = pl.ds(r, step)

                def entry(i, sums):
                    s1, s2, s3 = sums
                    src = inter_source[b, i]
                    shift = inter_shift[b, i]
                    s1 = s1 + tables[0, shift] * x[c][2, src, block]
                    s2 = s2 + tables[1, shift] * x[c][1, src, block]
                    s3 = s3 + tables[2, shift] * x[c][0, src, block]
                    return s1, s2, s3

                zero = jnp.zeros((step, 8, k_size), jnp.float32)
                s1, s2, s3 = lax.fori_loop(0, ni, entry, (zero, zero, zero), unroll=4)
                here = slice(bb * rc + 8 * r, bb * rc + 8 * (r + step))
                inc[c][here, :k_size] = (s1 - s2).reshape(8 * step, k_size)
                inc[c][here, k_size:] = (s1 + s3).reshape(8 * step, k_size)
        w = dot3(split(inc[c][...]), (dis_hi[...], dis_lo[...]))
        far_out[c][owner, 0] = w[:, :p_size].reshape(box_dev, rc, p_size)
        far_out[c][owner, 1] = w[:, p_size:].reshape(box_dev, rc, p_size)

    for c, (nz, rc, off) in enumerate(chunks):
        for turn, side in enumerate((y, 1 - y)):
            @pl.loop(1, zs)
            def _(o):
                peer = 2 * lax.rem(z + o, zs) + side
                line_copy(c, peer, peer).wait_recv()
                forward(c, peer)
                split_near((2 * c + turn) * (zs - 1) + o - 1)

        if nz == zs:
            na_copy(c, y, across(me), across(me)).start()
            nr_copy(c, y, across(partner), across(partner)).start()

        @pl.loop(0, dirs)
        def _(d):
            @pl.when(passes_on(d))
            def _():
                ng_copy(c, d, me).start()

        if c == 0:
            if shares > 1:
                @pl.loop(1, slabs)
                def _(o):
                    peer = lax.rem(slab + slabs - o, slabs)
                    ts_copy(peer, peer).wait_recv()

            turned = trans_all[...].reshape(k_size, 2 * nt).T
            rows[0] = turned[:nt]
            rows[1] = turned[:nt] + turned[nt:]
            rows[2] = turned[nt:] - turned[:nt]

            @pl.loop(0, nt)
            def _(t):
                for f in range(3):
                    tables[f, t] = jnp.broadcast_to(rows[f, pl.ds(t, 1), :], (8, k_size))

        radiate(c, 1)

        @pl.when(has_prev)
        def _():
            @pl.loop(0, dirs)
            def _(d):
                slab_copy(c, 0, d).wait_recv()

        radiate(c, 0)

        @pl.when(has_next)
        def _():
            @pl.loop(0, dirs)
            def _(d):
                slab_copy(c, 1, d).wait_recv()

        radiate(c, 2)
        group = 2 * nz
        base = me // group * group

        @pl.loop(0, group)
        def _(o):
            owner = base + 2 * lax.rem(toward(1 + o // 2), nz) + lax.rem(y + 1 + o, 2)
            far_device(c, owner)

            @pl.when(owner != me)
            def _():
                ret_copy(c, owner, me).start()

        far_all[:, :, my_rows(c, y, z)] = far_out[c][me]

    def near_weights(group, b, real, imag):
        w_hi[group * box_dev + b], w_lo[group * box_dev + b] = split(complex_weights(real, imag))

    for side in range(2):
        @pl.when(y == side)
        def _():
            for part in range(2):
                for b in range(box_dev):
                    near_par[part, b, :, side * hr:(side + 1) * hr] = par_t[part, b].T

    nb_copy(1 - y).wait_recv()
    for b in range(box_dev):
        near_weights(1, b, cur[0, b], cur[1, b])
        near_weights(2 - 2 * y, b, near_par[0, b], near_par[1, b])

    for c, (nz, rc, off) in enumerate(chunks):
        near_turned[:, :, my_rows(c, y, z)] = cells[c][1, across(me)]

        @pl.loop(0, 2 * zh)
        def _(o):
            holder = z // zh * zh * 2 + o

            @pl.when(holder != me)
            def _():
                ng_copy(c, across(me), holder).wait_recv()

        if nz == zs:
            na_copy(c, 1 - y, me, across(me)).wait_recv()
            nr_copy(c, y, me, across(me)).wait_recv()

    for b in range(box_dev):
        near_weights(2 * y, b, near_turned[0, b].T, near_turned[1, b].T)

    @pl.loop(0, box_dev)
    def _(b):
        total = jnp.zeros((p_size, 2 * illum), jnp.float32)
        for j in range(nn):
            src = near_index[b, j]
            total = total + dot3((near_hi[b, j], near_lo[b, j]), (w_hi[src], w_lo[src]))
        out[0, b] = total[:, :illum]
        out[1, b] = total[:, illum:]

    for c, (nz, rc, off) in enumerate(chunks):
        group = 2 * nz
        base = me // group * group

        @pl.loop(1, group)
        def _(o):
            peer = base + lax.rem(me + group - o, group)
            ret_copy(c, peer, peer).wait_recv()

    for part in range(2):
        for b in range(box_dev):
            out[part, b] += far_all[part, b].T

    for c, (nz, rc, off) in enumerate(chunks):
        group = 2 * nz
        base = me // group * group

        @pl.loop(1, group)
        def _(o):
            ret_copy(c, base + lax.rem(me + o, group), me).wait_send()

        @pl.loop(0, nz)
        def _(i):
            first_copy(c, i, 1 - y).wait_send()

        @pl.loop(1, zs)
        def _(o):
            peer = 2 * lax.rem(z + o, zs) + y
            line_copy(c, peer, me).wait_send()
            relay_copy(c, peer, partner).wait_send()

        @pl.loop(0, dirs)
        def _(d):
            @pl.when(passes_on(d))
            def _():
                ng_copy(c, d, me).wait_send()

        if nz == zs:
            na_copy(c, y, across(me), across(me)).wait_send()
            nr_copy(c, y, across(partner), across(partner)).wait_send()

        @pl.when(has_next)
        def _():
            @pl.loop(0, dirs)
            def _(d):
                slab_copy(c, 0, d).wait_send()

        @pl.when(has_prev)
        def _():
            @pl.loop(0, dirs)
            def _(d):
                slab_copy(c, 1, d).wait_send()

    @pl.loop(1, dirs)
    def _(o):
        tr_copy(lax.rem(me + o, dirs), me).wait_send()

    if shares > 1:
        @pl.loop(1, slabs)
        def _(o):
            ts_copy(lax.rem(slab + o, slabs), slab).wait_send()

    nb_copy(y).wait_send()


def body(slabs, dirs, *args):
    cur, near_blocks, near_index, aggregate, trans, inter_source, inter_shift, disaggregate = args
    box_dev, p_size, illum = cur.shape[1:]
    nn = near_blocks.shape[2]
    k_size = aggregate.shape[1]
    nt, k_loc = trans.shape[1:]
    slab_boxes = inter_source.shape[0]
    zs = dirs // 2
    chunks = plan(illum, zs)
    n = len(chunks)
    shares = slabs if k_loc % (8 * slabs) == 0 else 1
    f32, bf16 = jnp.float32, jnp.bfloat16
    vmem = pl.BlockSpec(memory_space=pltpu.VMEM)
    sem = pltpu.SemaphoreType.DMA
    turned = pltpu.VMEM((2, box_dev, illum, p_size), f32)
    operands = (
        cur, near_blocks, near_index, aggregate, jnp.swapaxes(trans, 1, 2), inter_source, inter_shift, disaggregate
    )
    return pl.pallas_call(
        functools.partial(kernel, slabs, dirs, chunks),
        out_shape=jax.ShapeDtypeStruct(cur.shape, f32),
        in_specs=[pl.BlockSpec(memory_space=pltpu.HBM)] * 8,
        out_specs=vmem,
        scratch_shapes=[
            pltpu.VMEM(cur.shape, f32),
            pltpu.SMEM(near_index.shape, jnp.int32),
            pltpu.VMEM(aggregate.shape, f32),
            pltpu.VMEM((2, k_loc, nt), f32),
            pltpu.SMEM(inter_source.shape, jnp.int32),
            pltpu.SMEM(inter_shift.shape, jnp.int32),
            pltpu.VMEM(disaggregate.shape, f32),
            sem((8,)),
            pltpu.VMEM(near_blocks.shape, f32),
            pltpu.VMEM((box_dev, nn, p_size, 2 * p_size), bf16),
            pltpu.VMEM((box_dev, nn, p_size, 2 * p_size), bf16),
            pltpu.VMEM(cur.shape, f32),
            turned,
            pltpu.VMEM((3 * box_dev, 2 * p_size, 2 * illum), bf16),
            pltpu.VMEM((3 * box_dev, 2 * p_size, 2 * illum), bf16),
            turned,
            pltpu.VMEM((2, box_dev, illum // 2, p_size), f32),
            turned,
            pltpu.VMEM((shares, k_loc // shares, 2 * nt), f32),
            pltpu.VMEM((dirs, shares, k_loc // shares, 2 * nt), f32),
            pltpu.VMEM((3, nt, k_size), f32),
            pltpu.VMEM((3, nt, 8, k_size), f32),
            pltpu.VMEM((2 * p_size, 2 * k_size), bf16),
            pltpu.VMEM((2 * p_size, 2 * k_size), bf16),
            pltpu.VMEM((2 * k_size, 2 * p_size), bf16),
            pltpu.VMEM((2 * k_size, 2 * p_size), bf16),
            [pltpu.VMEM((3, dirs, 2, box_dev, rc, p_size), f32) for _, rc, _ in chunks],
            [pltpu.VMEM((3, 3 * slab_boxes, rc // 8, 8, k_size), f32) for _, rc, _ in chunks],
            [pltpu.VMEM((box_dev * rc, 2 * k_size), f32) for _, rc, _ in chunks],
            [pltpu.VMEM((dirs, 2, box_dev, rc, p_size), f32) for _, rc, _ in chunks],
            pltpu.SemaphoreType.REGULAR((zs, 2)),
            sem((n, zs)), sem((n, zs)),
            sem((n, zs)), sem((n, zs)), sem((n, dirs)),
            sem((n, 2, dirs)), sem((n, 2, dirs)),
            sem((dirs,)), sem((dirs,)),
            sem((slabs,)), sem((slabs,)),
            sem(()), sem(()),
            sem((n, dirs)), sem((n, dirs)),
            sem((n,)), sem((n,)),
            sem((n,)), sem((n,)),
            sem((n, dirs)), sem((n, dirs)),
        ],
        compiler_params=pltpu.CompilerParams(
            collective_id=0, has_side_effects=True, vmem_limit_bytes=48 * 2**20
        ),
    )(*[pltpu.with_memory_space_constraint(v, pltpu.HBM) for v in operands])


def solution(mesh):
    in_specs = (
        P(None, ("slab", "dir"), None, None),
        P(None, ("slab", "dir"), None, None, None),
        P(("slab", "dir"), None),
        P(),
        P(None, None, "dir"),
        P("slab", None),
        P("slab", None),
        P(),
    )
    out_specs = P(None, ("slab", "dir"), None, None)
    run = functools.partial(body, mesh.shape["slab"], mesh.shape["dir"])
    return jax.shard_map(run, mesh=mesh, in_specs=in_specs, out_specs=out_specs, check_vma=False)
```

time: 41.7 us -> 40.8 us (0.978)
  the two profiles are of different devices: /device:TPU:15 before, /device:TPU:0 now
where the time goes in v2:
time: 40.8 us; the launch traced here: 40.7 us
  Pallas kernels  39.9 us (98%)
  local copies, waits for them, and re-layouts  0.8 us (2%)
    pallas_call x1, Pallas kernels, body(): pl.pallas_call(functools.partial(kernel, slabs, dirs, chunks), out_shape=...  39.9 us

profile of v2, /device:TPU:0, one launch (start us, length us, event | category | flops | bytes accessed | tf_op | source)
XLA Modules:
  0.0 40.7 jit_solution(9839952150356881444)
XLA Ops:
  0.0 39.9 %shard_map.82 = f32[2,2,128,256]{3,2,1,0:T(8,128)S(1)} custom-call(f32[2,2,128,256]{3,2,1,0:T(8,128)} %cur_hbm.1, f32[2,2,9,128,128]{4,3,2,1,0:T(8,128)} %near_hbm.1, s32[2,9]{1,0:T(2,128)} %near_index_hbm.1, f32[2,256,128]{2,1,0:T(8,128)} %aggregate_hbm.1, f32[2,32,64]{2,1,0:T(8,128)} %bitcast.1, s32[16,32]{1,0:T(8,128)} %source_hbm.1, s32[16,32]{1,0:T(8,128)} %shift_hbm.1, ...), custom_call_target="tpu_custom_call" | custom-call | tf_op jit(solution)/shard_map/pallas_call | solution.py:552
  39.9 0.8 %copy.10 = f32[2,2,128,256]{3,2,1,0:T(8,128)} copy(f32[2,2,128,256]{3,2,1,0:T(8,128)S(1)} %shard_map.82) | data formatting | bytes 1048576

commit v3 on v2

--- a/solution.py
+++ b/solution.py
@@ -60,6 +60,7 @@
     zs = dirs // 2
     zh = zs // 2
     hr = illum // 2
+    rc0 = illum // dirs
     z = me // 2
     y = lax.rem(me, 2)
     partner = 2 * z + 1 - y
@@ -72,13 +73,6 @@
 
     def across(d):
         return lax.rem(d + 2 * lax.rem(d, 2) - 1 + dirs, dirs)
-
-    def row(c, side, i):
-        nz, rc, off = chunks[c]
-        return pl.multiple_of(side * hr + off + lax.rem(i, nz) * rc, 8)
-
-    def my_rows(c, side, i):
-        return pl.ds(row(c, side, i), chunks[c][1])
 
     barrier = pltpu.get_barrier_semaphore()
 
@@ -115,7 +109,9 @@
 
     for part in range(2):
         for b in range(box_dev):
-            own_t[part, b] = cur[part, b].T
+            turned = cur[part, b].T
+            for d in range(dirs):
+                own_t[d // zs, d % zs, part, b] = turned[d * rc0:(d + 1) * rc0]
     trans_copy.wait()
     trans_own[...] = jnp.concatenate([trans[0], trans[1]], axis=1).reshape(trans_own.shape)
 
@@ -126,19 +122,19 @@
 
     def first_copy(c, i, side):
         return remote(
-            own_t.at[:, :, my_rows(c, side, i)], par_t.at[:, :, my_rows(c, 0, i)],
+            own_t.at[side, i], par_t.at[i],
             first_send.at[c, i], first_recv.at[c, i], dir=partner,
         )
 
     def line_copy(c, peer, slot):
         return remote(
-            own_t.at[:, :, my_rows(c, y, peer // 2)], cells[c].at[1, slot],
+            own_t.at[y, peer // 2], cells[c].at[1, slot],
             line_send.at[c, peer // 2], line_recv.at[c, slot], dir=peer,
         )
 
     def relay_copy(c, peer, slot):
         return remote(
-            par_t.at[:, :, my_rows(c, 0, peer // 2)], cells[c].at[1, slot],
+            par_t.at[peer // 2], cells[c].at[1, slot],
             relay_send.at[c, peer // 2], line_recv.at[c, slot], dir=peer,
         )
 
@@ -167,30 +163,28 @@
 
     def ng_copy(c, d, holder):
         return remote(
-            cells[c].at[1, d], near_turned.at[:, :, my_rows(c, lax.rem(holder, 2), holder // 2)],
+            cells[c].at[1, d], near_turned.at[lax.rem(holder, 2), holder // 2],
             ng_send.at[c, d], ng_recv.at[c, holder], dir=across(d),
         )
 
-    def apart(c, side, target):
-        nz, rc, off = chunks[c]
-        start = off + (1 - target // 2 // zh) * zh * rc
-        return pl.ds(pl.multiple_of(side * hr + start, 8), zh * rc)
+    def apart(target):
+        return pl.ds((1 - target // 2 // zh) * zh, zh)
 
     def na_copy(c, side, target, peer):
-        window = apart(c, side, target)
-        return remote(
-            own_t.at[:, :, window], near_turned.at[:, :, window], na_send.at[c], na_recv.at[c], dir=peer
+        window = apart(target)
+        return remote(
+            own_t.at[side, window], near_turned.at[side, window], na_send.at[c], na_recv.at[c], dir=peer
         )
 
     def nr_copy(c, side, target, peer):
         return remote(
-            par_t.at[:, :, apart(c, 0, target)], near_turned.at[:, :, apart(c, side, target)],
+            par_t.at[apart(target)], near_turned.at[side, apart(target)],
             nr_send.at[c], nr_recv.at[c], dir=peer,
         )
 
     def ret_copy(c, peer, sender):
         return remote(
-            far_out[c].at[peer], far_all.at[:, :, my_rows(c, lax.rem(sender, 2), sender // 2)],
+            far_out[c].at[peer], far_all.at[lax.rem(sender, 2), sender // 2],
             ret_send.at[c, peer], ret_recv.at[c, sender], dir=peer,
         )
 
@@ -208,6 +202,15 @@
         @pl.when(has_prev)
         def _():
             slab_copy(c, 1, d).start()
+
+    def spare(c, inside):
+        @pl.when(same_half(across(me)) == inside)
+        def _():
+            na_copy(c, y, across(me), across(me)).start()
+
+        @pl.when(same_half(across(partner)) == inside)
+        def _():
+            nr_copy(c, y, across(partner), across(partner)).start()
 
     def stage(s):
         @pl.when(has_upper)
@@ -258,7 +261,7 @@
     along(1)
     nb_copy(y).start()
     for c in range(len(chunks)):
-        cells[c][1, me] = own_t[:, :, my_rows(c, y, z)]
+        cells[c][1, me] = own_t[y, z]
         forward(c, me)
     for o in range(2, zs):
         staged(o - 2)
@@ -282,7 +285,9 @@
                 def _():
                     relay_copy(c, 2 * (i + g * nz) + y, partner).start()
 
-        cells[c][1, partner] = par_t[:, :, my_rows(c, 0, z)]
+        if nz == zs:
+            spare(c, True)
+        cells[c][1, partner] = par_t[z]
         forward(c, partner)
 
     trans_all[me, share] = trans_own[share]
@@ -297,17 +302,25 @@
         for c in range(len(chunks)):
             cells[c][2] = jnp.zeros_like(cells[c][2])
 
-    @pl.loop(1, dirs)
-    def _(o):
-        peer = lax.rem(me + dirs - o, dirs)
-        tr_copy(peer, peer).wait_recv()
-
-    if shares > 1:
-        @pl.loop(1, slabs)
-        def _(o):
-            ts_copy(lax.rem(slab + o, slabs), slab).start()
-
-    steps = 2 * (zs - 1) * len(chunks)
+    lines = 2 * (zs - 1)
+    steps = lines * len(chunks)
+
+    def take(c, q):
+        peer = 2 * toward(1 + lax.rem(q, zs - 1)) + lax.rem(y + q // (zs - 1), 2)
+        line_copy(c, peer, peer).wait_recv()
+        forward(c, peer)
+        split_near(c * lines + q)
+
+    def near_starts():
+        for c, (nz, rc, off) in enumerate(chunks):
+            if nz == zs:
+                spare(c, False)
+
+            @pl.loop(0, dirs)
+            def _(d):
+                @pl.when(passes_on(d))
+                def _():
+                    ng_copy(c, d, me).start()
     load = -(-box_dev * nn // steps)
 
     def split_near(t):
@@ -316,6 +329,15 @@
             b, j = q // nn, lax.rem(q, nn)
             pair = jnp.concatenate([near_blocks[0, b, j], near_blocks[1, b, j]], axis=1)
             near_hi[b, j], near_lo[b, j] = split(pair)
+
+    def joined(ref, part, b):
+        return jnp.concatenate([ref[i, part, b] for i in range(zs)], axis=0).T
+
+    def whole(ref, part, b):
+        return jnp.concatenate([ref[d // zs, d % zs, part, b] for d in range(dirs)], axis=0).T
+
+    def near_weights(group, b, real, imag):
+        w_hi[group * box_dev + b], w_lo[group * box_dev + b] = split(complex_weights(real, imag))
 
     def radiate(c, g):
         rc = chunks[c][1]
@@ -358,23 +380,27 @@
         far_out[c][owner, 1] = w[:, p_size:].reshape(box_dev, rc, p_size)
 
     for c, (nz, rc, off) in enumerate(chunks):
-        for turn, side in enumerate((y, 1 - y)):
-            @pl.loop(1, zs)
+        if c == 0:
+            @pl.loop(0, zs - 1)
+            def _(q):
+                take(0, q)
+
+            @pl.loop(1, dirs)
             def _(o):
-                peer = 2 * lax.rem(z + o, zs) + side
-                line_copy(c, peer, peer).wait_recv()
-                forward(c, peer)
-                split_near((2 * c + turn) * (zs - 1) + o - 1)
-
-        if nz == zs:
-            na_copy(c, y, across(me), across(me)).start()
-            nr_copy(c, y, across(partner), across(partner)).start()
-
-        @pl.loop(0, dirs)
-        def _(d):
-            @pl.when(passes_on(d))
-            def _():
-                ng_copy(c, d, me).start()
+                peer = lax.rem(me + dirs - o, dirs)
+                tr_copy(peer, peer).wait_recv()
+
+            if shares > 1:
+                @pl.loop(1, slabs)
+                def _(o):
+                    ts_copy(lax.rem(slab + o, slabs), slab).start()
+
+            @pl.loop(zs - 1, lines)
+            def _(q):
+                take(0, q)
+
+        if c == len(chunks) - 1:
+            near_starts()
 
         if c == 0:
             if shares > 1:
@@ -395,6 +421,19 @@
 
         radiate(c, 1)
 
+        if c == 0:
+            for side in range(2):
+                @pl.when(y == side)
+                def _():
+                    for part in range(2):
+                        for b in range(box_dev):
+                            near_par[part, b, :, side * hr:(side + 1) * hr] = joined(par_t, part, b)
+
+            nb_copy(1 - y).wait_recv()
+            for b in range(box_dev):
+                near_weights(1, b, cur[0, b], cur[1, b])
+                near_weights(2 - 2 * y, b, near_par[0, b], near_par[1, b])
+
         @pl.when(has_prev)
         def _():
             @pl.loop(0, dirs)
@@ -422,25 +461,17 @@
             def _():
                 ret_copy(c, owner, me).start()
 
-        far_all[:, :, my_rows(c, y, z)] = far_out[c][me]
-
-    def near_weights(group, b, real, imag):
-        w_hi[group * box_dev + b], w_lo[group * box_dev + b] = split(complex_weights(real, imag))
-
-    for side in range(2):
-        @pl.when(y == side)
-        def _():
-            for part in range(2):
-                for b in range(box_dev):
-                    near_par[part, b, :, side * hr:(side + 1) * hr] = par_t[part, b].T
-
-    nb_copy(1 - y).wait_recv()
-    for b in range(box_dev):
-        near_weights(1, b, cur[0, b], cur[1, b])
-        near_weights(2 - 2 * y, b, near_par[0, b], near_par[1, b])
+            if c + 1 < len(chunks):
+                each = -(-lines // group)
+
+                @pl.loop(o * each, jnp.minimum((o + 1) * each, lines))
+                def _(q):
+                    take(c + 1, q)
+
+        far_all[y, z] = far_out[c][me]
 
     for c, (nz, rc, off) in enumerate(chunks):
-        near_turned[:, :, my_rows(c, y, z)] = cells[c][1, across(me)]
+        near_turned[y, z] = cells[c][1, across(me)]
 
         @pl.loop(0, 2 * zh)
         def _(o):
@@ -455,7 +486,7 @@
             nr_copy(c, y, me, across(me)).wait_recv()
 
     for b in range(box_dev):
-        near_weights(2 * y, b, near_turned[0, b].T, near_turned[1, b].T)
+        near_weights(2 * y, b, whole(near_turned, 0, b), whole(near_turned, 1, b))
 
     @pl.loop(0, box_dev)
     def _(b):
@@ -477,7 +508,7 @@
 
     for part in range(2):
         for b in range(box_dev):
-            out[part, b] += far_all[part, b].T
+            out[part, b] += whole(far_all, part, b)
 
     for c, (nz, rc, off) in enumerate(chunks):
         group = 2 * nz
@@ -545,7 +576,7 @@
     f32, bf16 = jnp.float32, jnp.bfloat16
     vmem = pl.BlockSpec(memory_space=pltpu.VMEM)
     sem = pltpu.SemaphoreType.DMA
-    turned = pltpu.VMEM((2, box_dev, illum, p_size), f32)
+    turned = pltpu.VMEM((2, zs, 2, box_dev, illum // dirs, p_size), f32)
     operands = (
         cur, near_blocks, near_index, aggregate, jnp.swapaxes(trans, 1, 2), inter_source, inter_shift, disaggregate
     )
@@ -571,7 +602,7 @@
             pltpu.VMEM((3 * box_dev, 2 * p_size, 2 * illum), bf16),
             pltpu.VMEM((3 * box_dev, 2 * p_size, 2 * illum), bf16),
             turned,
-            pltpu.VMEM((2, box_dev, illum // 2, p_size), f32),
+            pltpu.VMEM((zs, 2, box_dev, illum // dirs, p_size), f32),
             turned,
             pltpu.VMEM((shares, k_loc // shares, 2 * nt), f32),
             pltpu.VMEM((dirs, shares, k_loc // shares, 2 * nt), f32),

time: 40.8 us -> 40 us (0.980)
  Pallas kernels: 39.9 us -> 39 us
    pallas_call x1, Pallas kernels: 39.9 us -> 39 us  [body(): pl.pallas_call(functools.partial(kernel, slabs, dirs, chunks), out_shape=...]
where the time goes in v3:
time: 40 us; the launch traced here: 39.9 us
  Pallas kernels  39 us (98%)
  local copies, waits for them, and re-layouts  0.8 us (2%)
    pallas_call x1, Pallas kernels, body(): pl.pallas_call(functools.partial(kernel, slabs, dirs, chunks), out_shape=...  39 us

profile of v3, /device:TPU:0, one launch (start us, length us, event | category | flops | bytes accessed | tf_op | source)
XLA Modules:
  0.0 39.9 jit_solution(13167371475326022133)
XLA Ops:
  0.0 39.0 %shard_map.82 = f32[2,2,128,256]{3,2,1,0:T(8,128)S(1)} custom-call(f32[2,2,128,256]{3,2,1,0:T(8,128)} %cur_hbm.1, f32[2,2,9,128,128]{4,3,2,1,0:T(8,128)} %near_hbm.1, s32[2,9]{1,0:T(2,128)} %near_index_hbm.1, f32[2,256,128]{2,1,0:T(8,128)} %aggregate_hbm.1, f32[2,32,64]{2,1,0:T(8,128)} %bitcast.1, s32[16,32]{1,0:T(8,128)} %source_hbm.1, s32[16,32]{1,0:T(8,128)} %shift_hbm.1, ...), custom_call_target="tpu_custom_call" | custom-call | tf_op jit(solution)/shard_map/pallas_call | solution.py:583
  39.1 0.8 %copy.10 = f32[2,2,128,256]{3,2,1,0:T(8,128)} copy(f32[2,2,128,256]{3,2,1,0:T(8,128)S(1)} %shard_map.82) | data formatting | bytes 1048576

commit v4 on v3

--- a/solution.py
+++ b/solution.py
@@ -276,6 +276,14 @@
     agg_hi[...], agg_lo[...] = split(complex_weights(aggregate[0].T, aggregate[1].T))
     dis_hi[...], dis_lo[...] = split(complex_weights(disaggregate[0].T, disaggregate[1].T))
 
+    lines = 2 * (zs - 1)
+    steps = zs - 1
+
+    def take(c, q):
+        peer = 2 * toward(1 + lax.rem(q, zs - 1)) + lax.rem(y + q // (zs - 1), 2)
+        line_copy(c, peer, peer).wait_recv()
+        forward(c, peer)
+
     for c, (nz, rc, off) in enumerate(chunks):
         for o in range(nz):
             i = lax.rem(toward(o + 1), nz)
@@ -285,6 +293,9 @@
                 def _():
                     relay_copy(c, 2 * (i + g * nz) + y, partner).start()
 
+            if o < zs - 1:
+                take(0, o)
+
         if nz == zs:
             spare(c, True)
         cells[c][1, partner] = par_t[z]
@@ -301,15 +312,6 @@
     def _():
         for c in range(len(chunks)):
             cells[c][2] = jnp.zeros_like(cells[c][2])
-
-    lines = 2 * (zs - 1)
-    steps = lines * len(chunks)
-
-    def take(c, q):
-        peer = 2 * toward(1 + lax.rem(q, zs - 1)) + lax.rem(y + q // (zs - 1), 2)
-        line_copy(c, peer, peer).wait_recv()
-        forward(c, peer)
-        split_near(c * lines + q)
 
     def near_starts():
         for c, (nz, rc, off) in enumerate(chunks):
@@ -381,10 +383,6 @@
 
     for c, (nz, rc, off) in enumerate(chunks):
         if c == 0:
-            @pl.loop(0, zs - 1)
-            def _(q):
-                take(0, q)
-
             @pl.loop(1, dirs)
             def _(o):
                 peer = lax.rem(me + dirs - o, dirs)
@@ -398,6 +396,7 @@
             @pl.loop(zs - 1, lines)
             def _(q):
                 take(0, q)
+                split_near(q - zs + 1)
 
         if c == len(chunks) - 1:
             near_starts()

time: 40 us -> 39.5 us (0.988)
  Pallas kernels: 39 us -> 38.5 us
    pallas_call x1, Pallas kernels: 39 us -> 38.5 us  [body(): pl.pallas_call(functools.partial(kernel, slabs, dirs, chunks), out_shape=...]
where the time goes in v4:
time: 39.5 us; the launch traced here: 39.3 us
  Pallas kernels  38.5 us (97%)
  local copies, waits for them, and re-layouts  0.8 us (2%)
    pallas_call x1, Pallas kernels, body(): pl.pallas_call(functools.partial(kernel, slabs, dirs, chunks), out_shape=...  38.5 us
    unnamed x1, local copies, waits for them, and re-layouts  0.8 us

profile of v4, /device:TPU:0, one launch (start us, length us, event | category | flops | bytes accessed | tf_op | source)
XLA Modules:
  0.0 39.3 jit_solution(13168522214376910599)
XLA Ops:
  0.0 38.5 %shard_map.82 = f32[2,2,128,256]{3,2,1,0:T(8,128)S(1)} custom-call(f32[2,2,128,256]{3,2,1,0:T(8,128)} %cur_hbm.1, f32[2,2,9,128,128]{4,3,2,1,0:T(8,128)} %near_hbm.1, s32[2,9]{1,0:T(2,128)} %near_index_hbm.1, f32[2,256,128]{2,1,0:T(8,128)} %aggregate_hbm.1, f32[2,32,64]{2,1,0:T(8,128)} %bitcast.1, s32[16,32]{1,0:T(8,128)} %source_hbm.1, s32[16,32]{1,0:T(8,128)} %shift_hbm.1, ...), custom_call_target="tpu_custom_call" | custom-call | tf_op jit(solution)/shard_map/pallas_call | solution.py:582
  38.5 0.8 %copy.10 = f32[2,2,128,256]{3,2,1,0:T(8,128)} copy(f32[2,2,128,256]{3,2,1,0:T(8,128)S(1)} %shard_map.82) | data formatting | bytes 1048576
